TPU v7x, 32 devices: a whole 2x2x4 slice. The times are simulated.
32 devices in a mesh: ctx: 8 (over y, x, core), page: 4 (over z).
Axes of the slice: x: 2, y: 2, z: 4, core: 2. Of those that a mesh axis runs over, the one named last changes fastest.
Arguments:
- queries: bfloat16 [2048, 8192], P('ctx', 'page'), may hold values from -200 to 200
- keys: bfloat16 [2048, 512], P('ctx', 'page'), may hold values from -6 to 6
- values: bfloat16 [2048, 512], P('ctx', 'page'), may hold values from -6 to 6
- span_table: int32 [16], replicated, may hold values from 0 to 15, each once
- page_slots: int32 [16], replicated, may hold values from 0 to 15, each once
Outputs:
- attended: bfloat16 [2048, 8192], P('ctx', 'page')
- cache_pages: bfloat16 [16, 4, 2, 128, 128], P('ctx')
- cache_scales: float32 [16, 4, 2], P('ctx')
Inputs may be any that keep to these rules, and one draw needn't show every extreme that they name: Stored span i (rows i * 128 to (i + 1) * 128 - 1) holds prompt positions span_table[i] * 128 onward; every value appears once. `page_slots`: every slot is named by exactly one page.
All inputs are finite; a program needn't handle non-finite values. Where the computation divides by a largest or mean magnitude, that divisor is 1e-20 or more.
Results may differ from a plain program's by a relative error of at most 0.0055.
Values may be sent and summed in bfloat16 or wider, within the bound.
A program may use at most 64 MiB of HBM per device.

v0:
```python
import math
import jax
import jax.numpy as jnp
from jax import lax
from jax.sharding import PartitionSpec as P

DH = 128
PAGE = 128
SPAN = 128


def on_device(queries, keys, values, span_table, page_slots):
    rows = queries.shape[0]
    kv_here = keys.shape[1] // DH
    q_here = queries.shape[1] // DH
    group = q_here // kv_here
    ctx_index = lax.axis_index("ctx")
    table_size = span_table.shape[0]
    scale = DH ** (-0.5)

    def token_positions(start, count):
        span_ids = start // SPAN + jnp.arange(count // SPAN, dtype=jnp.int32)
        onehot = span_ids[:, None] == jnp.arange(table_size, dtype=jnp.int32)[None, :]
        placed = jnp.sum(jnp.where(onehot, span_table[None, :], 0), axis=1)
        inner = jnp.arange(SPAN, dtype=jnp.int32)
        return (placed[:, None] * SPAN + inner[None, :]).reshape(count)

    query_pos = token_positions(ctx_index * rows, rows)
    query_heads = queries.reshape(rows, kv_here, group, DH)
    slots_here = rows // PAGE
    first_slot = ctx_index * slots_here
    page_ids = jnp.arange(page_slots.shape[0], dtype=jnp.int32)
    wanted = [
        jnp.sum(jnp.where(page_slots == first_slot + j, page_ids, 0)) for j in range(slots_here)
    ]

    def collect(held, piece):
        count = piece.shape[0]
        updated = []
        for j in range(slots_here):
            offset = wanted[j] * PAGE
            inside = (offset >= 0) & (offset + PAGE <= count)
            clamped = jnp.clip(offset, 0, count - PAGE)
            picked = lax.dynamic_slice_in_dim(piece, clamped, PAGE, 0)
            updated.append(jnp.where(inside, picked, held[j]))
        return jnp.stack(updated, axis=0)

    start_state = (
        jnp.full((kv_here, group, rows), -1e30, jnp.float32),
        jnp.zeros((kv_here, group, rows), jnp.float32),
        jnp.zeros((kv_here, group, rows, DH), jnp.float32),
    )
    empty_pages = jnp.zeros((slots_here, PAGE, kv_here * DH), jnp.bfloat16)
    state = start_state
    key_pages = empty_pages
    value_pages = empty_pages
    key_piece = lax.all_gather(keys, "ctx", axis=0, tiled=True)
    value_piece = lax.all_gather(values, "ctx", axis=0, tiled=True)
    count = key_piece.shape[0]
    key_pos = token_positions(jnp.int32(0), count)
    attend_state = state
    attend_key_piece = key_piece.reshape(count, kv_here, DH)
    attend_value_piece = value_piece.reshape(count, kv_here, DH)
    attend_count = attend_key_piece.shape[0]
    width = math.gcd(attend_count, 512)
    blocks = attend_count // width
    key_blocks = attend_key_piece.reshape(blocks, width, kv_here, DH)
    value_blocks = attend_value_piece.reshape(blocks, width, kv_here, DH)
    pos_blocks = key_pos.reshape(blocks, width)

    def step(carry, block):
        top, total, summed = carry
        key_block, value_block, pos_block = block
        score = (
            jnp.einsum("qhgd,khd->hgqk", query_heads, key_block, preferred_element_type=jnp.float32)
            * scale
        )
        keep = pos_block[None, :] <= query_pos[:, None]
        score = jnp.where(keep[None, None], score, -1e30)
        new_top = jnp.maximum(top, jnp.max(score, axis=-1))
        factor = jnp.exp(top - new_top)
        weight = jnp.where(keep[None, None], jnp.exp(score - new_top[..., None]), 0.0)
        total = total * factor + jnp.sum(weight, axis=-1)
        update = jnp.einsum(
            "hgqk,khd->hgqd",
            weight.astype(jnp.bfloat16),
            value_block,
            preferred_element_type=jnp.float32,
        )
        summed = summed * factor[..., None] + update
        return ((new_top, total, summed), None)

    attend_state, unused = lax.scan(step, attend_state, (key_blocks, value_blocks, pos_blocks))
    state = attend_state
    state, key_pages, value_pages = (
        state,
        collect(key_pages, key_piece),
        collect(value_pages, value_piece),
    )
    key_pages = key_pages.reshape(slots_here, PAGE, kv_here, DH).transpose(0, 2, 1, 3)
    value_pages = value_pages.reshape(slots_here, PAGE, kv_here, DH).transpose(0, 2, 1, 3)
    local_raw = jnp.stack([key_pages, value_pages], axis=2)
    raw = lax.all_gather(local_raw, "page", axis=1, tiled=True)
    top, total, summed = state
    result = summed / total[..., None]
    attended = jnp.transpose(result, (2, 0, 1, 3)).reshape(rows, q_here * DH).astype(jnp.bfloat16)
    raw_float = raw.astype(jnp.float32)
    cache_scales = jnp.max(jnp.abs(raw_float), axis=(3, 4)) + 1e-06
    cache_pages = (raw_float / cache_scales[..., None, None]).astype(jnp.bfloat16)
    return (attended, cache_pages, cache_scales)


def solution(mesh):
    placed = (P("ctx", "page"), P("ctx", "page"), P("ctx", "page"), P(), P())
    return jax.shard_map(
        on_device,
        mesh=mesh,
        in_specs=placed,
        out_specs=(P("ctx", "page"), P("ctx", None, None, None, None), P("ctx", None, None)),
        check_vma=False,
    )
```

profile of v0, /device:TPU:0, one launch (start us, length us, event | category | flops | bytes accessed | tf_op | source)
XLA Modules:
  0.0 111.6 jit_solution(16091338165210521844)
XLA Ops:
  0.7 0.8 select_reduce_fusion
  1.4 0.1 mul.56
  1.5 0.1 broadcast_bitcast_fusion
  1.6 11.6 %all_gather.9 = bf16[2048,128]{1,0:T(8,128)(2,1)S(1)} all-gather(bf16[256,128]{1,0:T(8,128)(2,1)} %param.8), channel_id=1, replica_groups=mesh['ctx'=8,'page'=4] {'ctx'}, dimensions={0}, use_global_device_ids=true | all-gather | bytes 589824 | tf_op jit(solution)/shard_map/all_gather | solution.py:57
  13.2 1.5 %copy.31 = bf16[256,2048]{0,1:T(8,128)(2,1)S(1)} copy(bf16[256,2048]{1,0:T(8,128)(2,1)} %param.7) | data formatting | bytes 2097152 | tf_op args[0]
  14.7 0.7 copy.33
  15.4 9.5 %all_gather.10 = bf16[2048,128]{1,0:T(8,128)(2,1)S(1)} all-gather(bf16[256,128]{1,0:T(8,128)(2,1)} %param.9), channel_id=1, replica_groups=mesh['ctx'=8,'page'=4] {'ctx'}, dimensions={0}, use_global_device_ids=true | all-gather | bytes 589824 | tf_op jit(solution)/shard_map/all_gather | solution.py:58
  24.9 0.8 fusion.26
  25.8 0.0 copy-start.1
  25.8 61.7 %while.15 = (s32[]{:T(128)}, f32[1,16,256]{2,1,0:T(8,128)S(1)}, f32[1,16,256]{2,1,0:T(8,128)S(1)}, f32[1,16,256,128]{3,2,1,0:T(8,128)}, s32[4,512]{1,0:T(4,128)S...) while((s32[]{:T(128)}, f32[1,16,256]{2,1,0:T(8,128)S(1)}, ...), condition=%wide.region_5.6_spmd.clone, body=%wide.region_2.5_spmd.clone.sunk | while | flops 1102733568 | bytes 65020080 | solution.py:93
  25.8 0.1 add_bitcast_fusion.2
  25.9 0.1 broadcast_compare_fusion.2
  26.0 4.6 %fusion.36 = (f32[16,256]{1,0:T(8,128)S(1)}, f32[512,256,16]{1,0,2:T(8,128)}) fusion(pred[256,512]{0,1:T(8,128)(4,1)S(1)} %broadcast_compare_fusion.2, bf16[256,1,16,128]{3,0,2,1:T(8,128)(2,1)S(1)} %get-tuple-element.249, bf16[4,512,1,128]{3,1,2,0:T(8,128)(2,1)S(1)} %get-tuple-element.248, s32[]{:T(128)S(6)} %copy.48), kind=kOutput, calls=%fused_computation.3.clone.1 | convolution fusion | flops 543158272 | bytes 9715716 | tf_op jit(solution)/shard_map/while/body/eval_jaxpr/qhgd,khd->hgqk/dot_general | solution.py:75
  30.6 0.0 copy-start
  30.6 4.6 %fusion.38 = f32[16,256]{1,0:T(8,128)S(1)} fusion(f32[512,256,16]{1,0,2:T(8,128)} %get-tuple-element.219, f32[16,256]{1,0:T(8,128)S(1)} %bitcast.114, pred[256,512]{0,1:T(8,128)(4,1)S(1)} %broadcast_compare_fusion.2), kind=kLoop, calls=%fused_computation.5.clone.1 | loop fusion | flops 10481664 | bytes 8552448 | tf_op jit(solution)/shard_map/while/body/eval_jaxpr/reduce_sum | solution.py:83
  35.2 1.2 %copy-done = f32[512,256,16]{1,0,2:T(8,128)S(1)} copy-done((f32[512,256,16]{1,0,2:T(8,128)S(1)}, f32[512,256,16]{1,0,2:T(8,128)}, u32[]{:S(2)}) %copy-start) | copy-done | bytes 8388632 | tf_op jit(solution)/shard_map/while
  36.4 3.9 %bitcast_add_fusion.6 = f32[1,16,256,128]{3,2,1,0:T(8,128)} fusion(f32[1,16,256,128]{3,2,1,0:T(8,128)} %get-tuple-element.235, f32[512,256,16]{1,0,2:T(8,128)S(1)} %copy-done, f32[16,256]{1,0:T(8,128)S(1)} %bitcast.115, pred[256,512]{0,1:T(8,128)(4,1)S(1)} %broadcast_compare_fusion.2, f32[16,256]{1,0:T(8,128)S(1)} %get-tuple-element.220, ...), kind=kOutput, calls=%fused_computation.9.clone.1 | convolution fusion | flops 548929536 | bytes 12877829 | tf_op jit(solution)/shard_map/while/body/eval_jaxpr/hgqk,khd->hgqd/dot_general | solution.py:84
  40.3 0.1 add_bitcast_fusion.2
  40.4 0.1 broadcast_compare_fusion.2
  40.5 4.6 %fusion.36 = (f32[16,256]{1,0:T(8,128)S(1)}, f32[512,256,16]{1,0,2:T(8,128)}) fusion(pred[256,512]{0,1:T(8,128)(4,1)S(1)} %broadcast_compare_fusion.2, bf16[256,1,16,128]{3,0,2,1:T(8,128)(2,1)S(1)} %get-tuple-element.249, bf16[4,512,1,128]{3,1,2,0:T(8,128)(2,1)S(1)} %get-tuple-element.248, s32[]{:T(128)S(6)} %copy.48), kind=kOutput, calls=%fused_computation.3.clone.1 | convolution fusion | flops 543158272 | bytes 9715716 | tf_op jit(solution)/shard_map/while/body/eval_jaxpr/qhgd,khd->hgqk/dot_general | solution.py:75
  45.1 0.0 copy-start
  45.1 4.6 %fusion.38 = f32[16,256]{1,0:T(8,128)S(1)} fusion(f32[512,256,16]{1,0,2:T(8,128)} %get-tuple-element.219, f32[16,256]{1,0:T(8,128)S(1)} %bitcast.114, pred[256,512]{0,1:T(8,128)(4,1)S(1)} %broadcast_compare_fusion.2), kind=kLoop, calls=%fused_computation.5.clone.1 | loop fusion | flops 10481664 | bytes 8552448 | tf_op jit(solution)/shard_map/while/body/eval_jaxpr/reduce_sum | solution.py:83
  49.7 1.2 %copy-done = f32[512,256,16]{1,0,2:T(8,128)S(1)} copy-done((f32[512,256,16]{1,0,2:T(8,128)S(1)}, f32[512,256,16]{1,0,2:T(8,128)}, u32[]{:S(2)}) %copy-start) | copy-done | bytes 8388632 | tf_op jit(solution)/shard_map/while
  50.9 5.1 %bitcast_add_fusion.6 = f32[1,16,256,128]{3,2,1,0:T(8,128)} fusion(f32[1,16,256,128]{3,2,1,0:T(8,128)} %get-tuple-element.235, f32[512,256,16]{1,0,2:T(8,128)S(1)} %copy-done, f32[16,256]{1,0:T(8,128)S(1)} %bitcast.115, pred[256,512]{0,1:T(8,128)(4,1)S(1)} %broadcast_compare_fusion.2, f32[16,256]{1,0:T(8,128)S(1)} %get-tuple-element.220, ...), kind=kOutput, calls=%fused_computation.9.clone.1 | convolution fusion | flops 548929536 | bytes 12877829 | tf_op jit(solution)/shard_map/while/body/eval_jaxpr/hgqk,khd->hgqd/dot_general | solution.py:84
  56.0 0.1 add_bitcast_fusion.2
  56.1 0.1 broadcast_compare_fusion.2
  56.2 4.6 %fusion.36 = (f32[16,256]{1,0:T(8,128)S(1)}, f32[512,256,16]{1,0,2:T(8,128)}) fusion(pred[256,512]{0,1:T(8,128)(4,1)S(1)} %broadcast_compare_fusion.2, bf16[256,1,16,128]{3,0,2,1:T(8,128)(2,1)S(1)} %get-tuple-element.249, bf16[4,512,1,128]{3,1,2,0:T(8,128)(2,1)S(1)} %get-tuple-element.248, s32[]{:T(128)S(6)} %copy.48), kind=kOutput, calls=%fused_computation.3.clone.1 | convolution fusion | flops 543158272 | bytes 9715716 | tf_op jit(solution)/shard_map/while/body/eval_jaxpr/qhgd,khd->hgqk/dot_general | solution.py:75
  60.8 0.0 copy-start
  60.8 4.6 %fusion.38 = f32[16,256]{1,0:T(8,128)S(1)} fusion(f32[512,256,16]{1,0,2:T(8,128)} %get-tuple-element.219, f32[16,256]{1,0:T(8,128)S(1)} %bitcast.114, pred[256,512]{0,1:T(8,128)(4,1)S(1)} %broadcast_compare_fusion.2), kind=kLoop, calls=%fused_computation.5.clone.1 | loop fusion | flops 10481664 | bytes 8552448 | tf_op jit(solution)/shard_map/while/body/eval_jaxpr/reduce_sum | solution.py:83
  65.5 1.2 %copy-done = f32[512,256,16]{1,0,2:T(8,128)S(1)} copy-done((f32[512,256,16]{1,0,2:T(8,128)S(1)}, f32[512,256,16]{1,0,2:T(8,128)}, u32[]{:S(2)}) %copy-start) | copy-done | bytes 8388632 | tf_op jit(solution)/shard_map/while
  66.6 5.1 %bitcast_add_fusion.6 = f32[1,16,256,128]{3,2,1,0:T(8,128)} fusion(f32[1,16,256,128]{3,2,1,0:T(8,128)} %get-tuple-element.235, f32[512,256,16]{1,0,2:T(8,128)S(1)} %copy-done, f32[16,256]{1,0:T(8,128)S(1)} %bitcast.115, pred[256,512]{0,1:T(8,128)(4,1)S(1)} %broadcast_compare_fusion.2, f32[16,256]{1,0:T(8,128)S(1)} %get-tuple-element.220, ...), kind=kOutput, calls=%fused_computation.9.clone.1 | convolution fusion | flops 548929536 | bytes 12877829 | tf_op jit(solution)/shard_map/while/body/eval_jaxpr/hgqk,khd->hgqd/dot_general | solution.py:84
  71.7 0.1 add_bitcast_fusion.2
  71.8 0.1 broadcast_compare_fusion.2
  72.0 4.6 %fusion.36 = (f32[16,256]{1,0:T(8,128)S(1)}, f32[512,256,16]{1,0,2:T(8,128)}) fusion(pred[256,512]{0,1:T(8,128)(4,1)S(1)} %broadcast_compare_fusion.2, bf16[256,1,16,128]{3,0,2,1:T(8,128)(2,1)S(1)} %get-tuple-element.249, bf16[4,512,1,128]{3,1,2,0:T(8,128)(2,1)S(1)} %get-tuple-element.248, s32[]{:T(128)S(6)} %copy.48), kind=kOutput, calls=%fused_computation.3.clone.1 | convolution fusion | flops 543158272 | bytes 9715716 | tf_op jit(solution)/shard_map/while/body/eval_jaxpr/qhgd,khd->hgqk/dot_general | solution.py:75
  76.5 0.0 copy-start
  76.5 4.6 %fusion.38 = f32[16,256]{1,0:T(8,128)S(1)} fusion(f32[512,256,16]{1,0,2:T(8,128)} %get-tuple-element.219, f32[16,256]{1,0:T(8,128)S(1)} %bitcast.114, pred[256,512]{0,1:T(8,128)(4,1)S(1)} %broadcast_compare_fusion.2), kind=kLoop, calls=%fused_computation.5.clone.1 | loop fusion | flops 10481664 | bytes 8552448 | tf_op jit(solution)/shard_map/while/body/eval_jaxpr/reduce_sum | solution.py:83
  81.2 1.2 %copy-done = f32[512,256,16]{1,0,2:T(8,128)S(1)} copy-done((f32[512,256,16]{1,0,2:T(8,128)S(1)}, f32[512,256,16]{1,0,2:T(8,128)}, u32[]{:S(2)}) %copy-start) | copy-done | bytes 8388632 | tf_op jit(solution)/shard_map/while
  82.4 5.1 %bitcast_add_fusion.6 = f32[1,16,256,128]{3,2,1,0:T(8,128)} fusion(f32[1,16,256,128]{3,2,1,0:T(8,128)} %get-tuple-element.235, f32[512,256,16]{1,0,2:T(8,128)S(1)} %copy-done, f32[16,256]{1,0:T(8,128)S(1)} %bitcast.115, pred[256,512]{0,1:T(8,128)(4,1)S(1)} %broadcast_compare_fusion.2, f32[16,256]{1,0:T(8,128)S(1)} %get-tuple-element.220, ...), kind=kOutput, calls=%fused_computation.9.clone.1 | convolution fusion | flops 548929536 | bytes 12877829 | tf_op jit(solution)/shard_map/while/body/eval_jaxpr/hgqk,khd->hgqd/dot_general | solution.py:84
  87.5 1.9 %fusion.25 = bf16[256,1,16,128]{3,0,2,1:T(8,128)(2,1)S(1)} fusion(f32[1,16,256,128]{3,2,1,0:T(8,128)} %get-tuple-element.51, f32[16,256]{1,0:T(8,128)S(1)} %bitcast.123), kind=kLoop, calls=%fused_computation.36 | loop fusion | flops 1048576 | bytes 3162112 | tf_op jit(solution)/shard_map/convert_element_type | solution.py:106
  89.4 0.7 copy.35
  90.1 1.2 %copy.43 = bf16[32,8,16,128]{3,1,2,0:T(8,128)(2,1)} copy(bf16[32,8,16,128]{3,2,1,0:T(8,128)(2,1)S(1)} %bitcast.116) | data formatting | bytes 2097152
  91.3 0.0 copy-done.1
  91.3 0.6 fusion.27
  93.3 0.1 select_bitcast_fusion.1
  93.4 16.3 %all_gather.11 = bf16[2,4,2,128,128]{4,3,2,1,0:T(8,128)(2,1)S(1)} all-gather(bf16[2,1,2,128,128]{4,3,2,1,0:T(8,128)(2,1)S(1)} %pad_maximum_fusion), channel_id=1, replica_groups=mesh['ctx'=8,'page'=4] {'page'}, dimensions={1}, use_global_device_ids=true | all-gather | bytes 655360 | tf_op jit(solution)/shard_map/all_gather | solution.py:103
  109.8 0.2 fusion.23
  110.0 1.0 fusion.24
  111.0 0.7 copy.37
  (28 shorter events, 0.2 us)
Async XLA Ops:
  25.8 65.6 %copy-start.1 = (s32[16]{0:T(128)S(1)}, s32[16]{0:T(128)}, u32[]{:S(2)}) copy-start(s32[16]{0:T(128)} %param.11) | copy-start | bytes 196
  30.6 5.8 %copy-start = (f32[512,256,16]{1,0,2:T(8,128)S(1)}, f32[512,256,16]{1,0,2:T(8,128)}, u32[]{:S(2)}) copy-start(f32[512,256,16]{1,0,2:T(8,128)} %get-tuple-element.219) | copy-start | bytes 25165828 | tf_op jit(solution)/shard_map/while
  45.1 5.8 %copy-start = (f32[512,256,16]{1,0,2:T(8,128)S(1)}, f32[512,256,16]{1,0,2:T(8,128)}, u32[]{:S(2)}) copy-start(f32[512,256,16]{1,0,2:T(8,128)} %get-tuple-element.219) | copy-start | bytes 25165828 | tf_op jit(solution)/shard_map/while
  60.8 5.8 %copy-start = (f32[512,256,16]{1,0,2:T(8,128)S(1)}, f32[512,256,16]{1,0,2:T(8,128)}, u32[]{:S(2)}) copy-start(f32[512,256,16]{1,0,2:T(8,128)} %get-tuple-element.219) | copy-start | bytes 25165828 | tf_op jit(solution)/shard_map/while
  76.5 5.8 %copy-start = (f32[512,256,16]{1,0,2:T(8,128)S(1)}, f32[512,256,16]{1,0,2:T(8,128)}, u32[]{:S(2)}) copy-start(f32[512,256,16]{1,0,2:T(8,128)} %get-tuple-element.219) | copy-start | bytes 25165828 | tf_op jit(solution)/shard_map/while
where the time goes:
time: 112 us
  blocking collectives  37.5 us (33%)
  matrix products  37.4 us (33%)
  other arithmetic  24.8 us (22%)
  local copies, waits for them, and re-layouts  9.68 us (9%)
  between operations  2.05 us (2%)
    dot_general x4, matrix products, step(): jnp.einsum('hgqk,khd->hgqd', weight.astype(jnp.bfloat16), value_block, pr...  19.1 us
    reduce_sum x4, other arithmetic, step(): total = total * factor + jnp.sum(weight, axis=-1)  18.4 us
    dot_general x4, matrix products, step(): jnp.einsum('qhgd,khd->hgqk', query_heads, key_block, preferred_element_ty...  18.3 us
    all_gather x1, blocking collectives, on_device(): raw = lax.all_gather(local_raw, 'page', axis=1, tiled=True)  16.3 us
    all_gather x1, blocking collectives, on_device(): key_piece = lax.all_gather(keys, 'ctx', axis=0, tiled=True)  11.6 us
    all_gather x1, blocking collectives, on_device(): value_piece = lax.all_gather(values, 'ctx', axis=0, tiled=True)  9.53 us
    while x12, local copies, waits for them, and re-layouts  4.76 us
    unnamed x7, local copies, waits for them, and re-layouts  4.13 us

commit v1 on v0

--- a/solution.py
+++ b/solution.py
@@ -7,6 +7,13 @@
 DH = 128
 PAGE = 128
 SPAN = 128
+
+
+def _resolve_patches(a0, my_data, net_axis):
+    local_part = lax.all_gather(
+        jnp.concatenate([a0, my_data], axis=1), axis_name=net_axis, axis=0, tiled=True
+    )
+    return jnp.split(local_part, [a0.shape[1]], axis=1)
 
 
 def on_device(queries, keys, values, span_table, page_slots):
@@ -54,8 +61,7 @@
     state = start_state
     key_pages = empty_pages
     value_pages = empty_pages
-    key_piece = lax.all_gather(keys, "ctx", axis=0, tiled=True)
-    value_piece = lax.all_gather(values, "ctx", axis=0, tiled=True)
+    key_piece, value_piece = _resolve_patches(keys, values, "ctx")
     count = key_piece.shape[0]
     key_pos = token_positions(jnp.int32(0), count)
     attend_state = state

time: 112 us -> 129 us (1.15)
  blocking collectives: 37.5 us -> 16 us
  waiting for transfers between devices: 0 us -> 21 us
  between operations: 2.05 us -> 15.5 us
  other arithmetic: 24.8 us -> 27.1 us
    all_gather x2 -> x0, blocking collectives: 21.2 us -> none  [the longest x1 11.6 us: on_device(): key_piece = lax.all_gather(keys, 'ctx', axis=0, tiled=True)]
    all_gather x0 -> x1, waiting for transfers between devices: none -> 21 us  [_resolve_patches(): lax.all_gather(jnp.concatenate([a0, my_data], axis=1), axis_name=net_axis...]
    concatenate x0 -> x1, other arithmetic: none -> 1.54 us  [_resolve_patches(): jnp.concatenate([a0, my_data], axis=1)]
    unnamed x7 -> x5, local copies, waits for them, and re-layouts: 4.13 us -> 4.13 us
  transfers between devices with their start and end apart: 0 -> 1, of which waited for: 0 -> 1; matrix products, arithmetic and copies ran while one was open for 0% -> 4% of each run, Pallas kernels for 0% -> 0%
where the time goes in v1:
time: 129 us; the launch traced here: 128 us
  matrix products  37.4 us (29%)
  other arithmetic  27.1 us (21%)
  waiting for transfers between devices  21 us (16%)
  blocking collectives  16 us (12%)
  between operations  15.5 us (12%)
  local copies, waits for them, and re-layouts  10.9 us (8%)
    all_gather x1, waiting for transfers between devices, _resolve_patches(): lax.all_gather(jnp.concatenate([a0, my_data], axis=1), axis_name=net_axis...  21 us
    dot_general x4, matrix products, step(): jnp.einsum('hgqk,khd->hgqd', weight.astype(jnp.bfloat16), value_block, pr...  19.1 us
    reduce_sum x4, other arithmetic, step(): total = total * factor + jnp.sum(weight, axis=-1)  18.4 us
    dot_general x4, matrix products, step(): jnp.einsum('qhgd,khd->hgqk', query_heads, key_block, preferred_element_ty...  18.3 us
    all_gather x1, blocking collectives, on_device(): raw = lax.all_gather(local_raw, 'page', axis=1, tiled=True)  16 us
    while x12, local copies, waits for them, and re-layouts  4.76 us
    unnamed x5, local copies, waits for them, and re-layouts  4.13 us
  transfers between devices with their start and end apart: 1, of which 1 were waited for; matrix products, arithmetic and copies ran while one was open for 4% of the time, Pallas kernels for 0%

profile of v1, /device:TPU:0, one launch (start us, length us, event | category | flops | bytes accessed | tf_op | source)
XLA Modules:
  0.0 128.2 jit_solution(9111311375720837800)
XLA Ops:
  7.2 0.0 all-gather.2.cloned.1.call-start
  7.2 1.5 %pad_maximum_fusion = bf16[256,256]{1,0:T(8,128)(2,1)} fusion(bf16[256,128]{1,0:T(8,128)(2,1)} %param.9, bf16[256,128]{1,0:T(8,128)(2,1)} %param.8), kind=kLoop, calls=%fused_computation.37 | loop fusion | flops 262144 | bytes 262144 | tf_op jit(solution)/shard_map/concatenate | solution.py:14
  8.8 0.0 all-gather.2.cloned.1.call-update
  8.8 1.4 %fusion.27 = (s32[]{:T(128)}, s32[]{:T(128)}) fusion(s32[16]{0:T(128)} %param.11, s32[]{:T(128)S(6)} %mul.59, s32[]{:T(128)S(6)} %add.91), kind=kLoop, calls=%fused_computation.55 | loop fusion | flops 94 | bytes 80 | tf_op jit(solution)/shard_map/reduce_sum | solution.py:41
  11.5 0.8 select_reduce_fusion
  12.3 0.1 mul.56
  12.4 1.5 %copy.31 = bf16[256,2048]{0,1:T(8,128)(2,1)S(1)} copy(bf16[256,2048]{1,0:T(8,128)(2,1)} %param.7) | data formatting | bytes 2097152 | tf_op args[0]
  13.9 0.7 copy.33
  14.6 0.8 fusion.26
  15.5 0.1 broadcast_bitcast_fusion
  15.6 21.0 %all-gather.2.cloned.1.call-done = bf16[2048,256]{1,0:T(8,128)(2,1)} async-done(((bf16[256,256]{1,0:T(8,128)(2,1)}), bf16[2048,256]{1,0:T(8,128)(2,1)}) %all-gather.2.cloned.1.call-update) | async-done | bytes 1048592 | tf_op jit(solution)/shard_map/all_gather | solution.py:13
  36.6 1.3 fusion.29
  37.8 0.1 select_bitcast_fusion.1
  38.0 16.0 %all_gather.7 = bf16[2,4,2,128,128]{4,3,2,1,0:T(8,128)(2,1)S(1)} all-gather(bf16[2,1,2,128,128]{4,3,2,1,0:T(8,128)(2,1)S(1)} %pad_maximum_fusion.1), channel_id=1, replica_groups=mesh['ctx'=8,'page'=4] {'page'}, dimensions={1}, use_global_device_ids=true | all-gather | bytes 655360 | tf_op jit(solution)/shard_map/all_gather | solution.py:109
  54.0 0.2 fusion.23
  54.2 1.0 fusion.24
  55.2 0.7 copy.37
  55.8 61.7 %while.15 = (s32[]{:T(128)}, f32[1,16,256]{2,1,0:T(8,128)S(1)}, f32[1,16,256]{2,1,0:T(8,128)S(1)}, f32[1,16,256,128]{3,2,1,0:T(8,128)}, s32[4,512]{1,0:T(4,128)S...) while((s32[]{:T(128)}, f32[1,16,256]{2,1,0:T(8,128)S(1)}, ...), condition=%wide.region_5.6_spmd.clone, body=%wide.region_2.5_spmd.clone.sunk | while | flops 1102733568 | bytes 65020080 | solution.py:99
  55.8 0.1 add_bitcast_fusion.2
  55.9 0.1 broadcast_compare_fusion.2
  56.1 4.6 %fusion.37 = (f32[16,256]{1,0:T(8,128)S(1)}, f32[512,256,16]{1,0,2:T(8,128)}) fusion(pred[256,512]{0,1:T(8,128)(4,1)S(1)} %broadcast_compare_fusion.2, bf16[256,1,16,128]{3,0,2,1:T(8,128)(2,1)S(1)} %get-tuple-element.251, bf16[4,512,1,128]{3,1,2,0:T(8,128)(2,1)S(1)} %get-tuple-element.250, s32[]{:T(128)S(6)} %copy.48), kind=kOutput, calls=%fused_computation.3.clone.1 | convolution fusion | flops 543158272 | bytes 9715716 | tf_op jit(solution)/shard_map/while/body/eval_jaxpr/qhgd,khd->hgqk/dot_general | solution.py:81
  60.6 0.0 copy-start
  60.7 4.6 %fusion.39 = f32[16,256]{1,0:T(8,128)S(1)} fusion(f32[512,256,16]{1,0,2:T(8,128)} %get-tuple-element.221, f32[16,256]{1,0:T(8,128)S(1)} %bitcast.114, pred[256,512]{0,1:T(8,128)(4,1)S(1)} %broadcast_compare_fusion.2), kind=kLoop, calls=%fused_computation.5.clone.1 | loop fusion | flops 10481664 | bytes 8552448 | tf_op jit(solution)/shard_map/while/body/eval_jaxpr/reduce_sum | solution.py:89
  65.3 1.2 copy-done
  66.5 3.9 %bitcast_add_fusion.6 = f32[1,16,256,128]{3,2,1,0:T(8,128)} fusion(f32[1,16,256,128]{3,2,1,0:T(8,128)} %get-tuple-element.237, f32[512,256,16]{1,0,2:T(8,128)S(1)} %copy-done, f32[16,256]{1,0:T(8,128)S(1)} %bitcast.115, pred[256,512]{0,1:T(8,128)(4,1)S(1)} %broadcast_compare_fusion.2, f32[16,256]{1,0:T(8,128)S(1)} %get-tuple-element.222, ...), kind=kOutput, calls=%fused_computation.9.clone.1 | convolution fusion | flops 548929536 | bytes 12877829 | tf_op jit(solution)/shard_map/while/body/eval_jaxpr/hgqk,khd->hgqd/dot_general | solution.py:90
  70.3 0.1 add_bitcast_fusion.2
  70.4 0.1 broadcast_compare_fusion.2
  70.6 4.6 %fusion.37 = (f32[16,256]{1,0:T(8,128)S(1)}, f32[512,256,16]{1,0,2:T(8,128)}) fusion(pred[256,512]{0,1:T(8,128)(4,1)S(1)} %broadcast_compare_fusion.2, bf16[256,1,16,128]{3,0,2,1:T(8,128)(2,1)S(1)} %get-tuple-element.251, bf16[4,512,1,128]{3,1,2,0:T(8,128)(2,1)S(1)} %get-tuple-element.250, s32[]{:T(128)S(6)} %copy.48), kind=kOutput, calls=%fused_computation.3.clone.1 | convolution fusion | flops 543158272 | bytes 9715716 | tf_op jit(solution)/shard_map/while/body/eval_jaxpr/qhgd,khd->hgqk/dot_general | solution.py:81
  75.1 0.0 copy-start
  75.2 4.6 %fusion.39 = f32[16,256]{1,0:T(8,128)S(1)} fusion(f32[512,256,16]{1,0,2:T(8,128)} %get-tuple-element.221, f32[16,256]{1,0:T(8,128)S(1)} %bitcast.114, pred[256,512]{0,1:T(8,128)(4,1)S(1)} %broadcast_compare_fusion.2), kind=kLoop, calls=%fused_computation.5.clone.1 | loop fusion | flops 10481664 | bytes 8552448 | tf_op jit(solution)/shard_map/while/body/eval_jaxpr/reduce_sum | solution.py:89
  79.8 1.2 copy-done
  81.0 5.1 %bitcast_add_fusion.6 = f32[1,16,256,128]{3,2,1,0:T(8,128)} fusion(f32[1,16,256,128]{3,2,1,0:T(8,128)} %get-tuple-element.237, f32[512,256,16]{1,0,2:T(8,128)S(1)} %copy-done, f32[16,256]{1,0:T(8,128)S(1)} %bitcast.115, pred[256,512]{0,1:T(8,128)(4,1)S(1)} %broadcast_compare_fusion.2, f32[16,256]{1,0:T(8,128)S(1)} %get-tuple-element.222, ...), kind=kOutput, calls=%fused_computation.9.clone.1 | convolution fusion | flops 548929536 | bytes 12877829 | tf_op jit(solution)/shard_map/while/body/eval_jaxpr/hgqk,khd->hgqd/dot_general | solution.py:90
  86.1 0.1 add_bitcast_fusion.2
  86.1 0.1 broadcast_compare_fusion.2
  86.3 4.6 %fusion.37 = (f32[16,256]{1,0:T(8,128)S(1)}, f32[512,256,16]{1,0,2:T(8,128)}) fusion(pred[256,512]{0,1:T(8,128)(4,1)S(1)} %broadcast_compare_fusion.2, bf16[256,1,16,128]{3,0,2,1:T(8,128)(2,1)S(1)} %get-tuple-element.251, bf16[4,512,1,128]{3,1,2,0:T(8,128)(2,1)S(1)} %get-tuple-element.250, s32[]{:T(128)S(6)} %copy.48), kind=kOutput, calls=%fused_computation.3.clone.1 | convolution fusion | flops 543158272 | bytes 9715716 | tf_op jit(solution)/shard_map/while/body/eval_jaxpr/qhgd,khd->hgqk/dot_general | solution.py:81
  90.9 0.0 copy-start
  90.9 4.6 %fusion.39 = f32[16,256]{1,0:T(8,128)S(1)} fusion(f32[512,256,16]{1,0,2:T(8,128)} %get-tuple-element.221, f32[16,256]{1,0:T(8,128)S(1)} %bitcast.114, pred[256,512]{0,1:T(8,128)(4,1)S(1)} %broadcast_compare_fusion.2), kind=kLoop, calls=%fused_computation.5.clone.1 | loop fusion | flops 10481664 | bytes 8552448 | tf_op jit(solution)/shard_map/while/body/eval_jaxpr/reduce_sum | solution.py:89
  95.5 1.2 copy-done
  96.7 5.1 %bitcast_add_fusion.6 = f32[1,16,256,128]{3,2,1,0:T(8,128)} fusion(f32[1,16,256,128]{3,2,1,0:T(8,128)} %get-tuple-element.237, f32[512,256,16]{1,0,2:T(8,128)S(1)} %copy-done, f32[16,256]{1,0:T(8,128)S(1)} %bitcast.115, pred[256,512]{0,1:T(8,128)(4,1)S(1)} %broadcast_compare_fusion.2, f32[16,256]{1,0:T(8,128)S(1)} %get-tuple-element.222, ...), kind=kOutput, calls=%fused_computation.9.clone.1 | convolution fusion | flops 548929536 | bytes 12877829 | tf_op jit(solution)/shard_map/while/body/eval_jaxpr/hgqk,khd->hgqd/dot_general | solution.py:90
  101.8 0.1 add_bitcast_fusion.2
  101.9 0.1 broadcast_compare_fusion.2
  102.0 4.6 %fusion.37 = (f32[16,256]{1,0:T(8,128)S(1)}, f32[512,256,16]{1,0,2:T(8,128)}) fusion(pred[256,512]{0,1:T(8,128)(4,1)S(1)} %broadcast_compare_fusion.2, bf16[256,1,16,128]{3,0,2,1:T(8,128)(2,1)S(1)} %get-tuple-element.251, bf16[4,512,1,128]{3,1,2,0:T(8,128)(2,1)S(1)} %get-tuple-element.250, s32[]{:T(128)S(6)} %copy.48), kind=kOutput, calls=%fused_computation.3.clone.1 | convolution fusion | flops 543158272 | bytes 9715716 | tf_op jit(solution)/shard_map/while/body/eval_jaxpr/qhgd,khd->hgqk/dot_general | solution.py:81
  106.6 0.0 copy-start
  106.6 4.6 %fusion.39 = f32[16,256]{1,0:T(8,128)S(1)} fusion(f32[512,256,16]{1,0,2:T(8,128)} %get-tuple-element.221, f32[16,256]{1,0:T(8,128)S(1)} %bitcast.114, pred[256,512]{0,1:T(8,128)(4,1)S(1)} %broadcast_compare_fusion.2), kind=kLoop, calls=%fused_computation.5.clone.1 | loop fusion | flops 10481664 | bytes 8552448 | tf_op jit(solution)/shard_map/while/body/eval_jaxpr/reduce_sum | solution.py:89
  111.2 1.2 copy-done
  112.4 5.1 %bitcast_add_fusion.6 = f32[1,16,256,128]{3,2,1,0:T(8,128)} fusion(f32[1,16,256,128]{3,2,1,0:T(8,128)} %get-tuple-element.237, f32[512,256,16]{1,0,2:T(8,128)S(1)} %copy-done, f32[16,256]{1,0:T(8,128)S(1)} %bitcast.115, pred[256,512]{0,1:T(8,128)(4,1)S(1)} %broadcast_compare_fusion.2, f32[16,256]{1,0:T(8,128)S(1)} %get-tuple-element.222, ...), kind=kOutput, calls=%fused_computation.9.clone.1 | convolution fusion | flops 548929536 | bytes 12877829 | tf_op jit(solution)/shard_map/while/body/eval_jaxpr/hgqk,khd->hgqd/dot_general | solution.py:90
  117.5 1.9 %fusion.25 = bf16[256,1,16,128]{3,0,2,1:T(8,128)(2,1)S(1)} fusion(f32[1,16,256,128]{3,2,1,0:T(8,128)} %get-tuple-element.51, f32[16,256]{1,0:T(8,128)S(1)} %bitcast.121), kind=kLoop, calls=%fused_computation.36 | loop fusion | flops 1048576 | bytes 3162112 | tf_op jit(solution)/shard_map/convert_element_type | solution.py:112
  119.5 0.7 copy.35
  120.1 1.2 copy.43
  (28 shorter events, 0.2 us)
Async XLA Ops:
  7.2 29.4 %all-gather.2.cloned.1.call-start = ((), (), s32[]{:S(2)}) async-start(), calls=%async_computation | async-start | bytes 1179648 | tf_op jit(solution)/shard_map/all_gather | solution.py:13
  60.6 5.8 %copy-start = (f32[512,256,16]{1,0,2:T(8,128)S(1)}, f32[512,256,16]{1,0,2:T(8,128)}, u32[]{:S(2)}) copy-start(f32[512,256,16]{1,0,2:T(8,128)} %get-tuple-element.221) | copy-start | bytes 25165828 | tf_op jit(solution)/shard_map/while
  75.1 5.8 %copy-start = (f32[512,256,16]{1,0,2:T(8,128)S(1)}, f32[512,256,16]{1,0,2:T(8,128)}, u32[]{:S(2)}) copy-start(f32[512,256,16]{1,0,2:T(8,128)} %get-tuple-element.221) | copy-start | bytes 25165828 | tf_op jit(solution)/shard_map/while
  90.9 5.8 %copy-start = (f32[512,256,16]{1,0,2:T(8,128)S(1)}, f32[512,256,16]{1,0,2:T(8,128)}, u32[]{:S(2)}) copy-start(f32[512,256,16]{1,0,2:T(8,128)} %get-tuple-element.221) | copy-start | bytes 25165828 | tf_op jit(solution)/shard_map/while
  106.6 5.8 %copy-start = (f32[512,256,16]{1,0,2:T(8,128)S(1)}, f32[512,256,16]{1,0,2:T(8,128)}, u32[]{:S(2)}) copy-start(f32[512,256,16]{1,0,2:T(8,128)} %get-tuple-element.221) | copy-start | bytes 25165828 | tf_op jit(solution)/shard_map/while
Sparse Core Ops, SparseCore 0:
  10.4 26.0 all-gather.1
